TPU v7x, 512 devices: a whole 4x8x8 slice. The times are simulated.
512 devices in a mesh: tok: 8 (over z), row: 8 (over y_hi, core), col: 8 (over x, y_lo).
Axes of the slice: x: 4, y: 8 (y_hi: 4, y_lo: 2; y = y_hi * 2 + y_lo), z: 8, core: 2. Of those that a mesh axis runs over, the one named last changes fastest.
Arguments:
- activations: bfloat16 [2048, 8192], P('tok', 'row'), may hold values from -8 to 8
- gradients: bfloat16 [2048, 8192], P('tok', 'col'), may hold values from -8 to 8
- act_basis: bfloat16 [8192, 8192], P('row', ('tok', 'col')), may hold values from -1 to 1
- grad_basis: bfloat16 [8192, 8192], P('col', 'row'), may hold values from -1 to 1
- eigen_noise: float32 [8192, 8192], P('row', ('tok', 'col')), may hold values from -6 to 6
Outputs:
- scales: float32 [8192, 8192], P('row', ('tok', 'col'))
- output_shift: bfloat16 [2048, 8192], P('tok', 'col')
All inputs are finite; a program needn't handle non-finite values.
Results may differ from a plain program's by a relative error of at most 0.0064.
Values may be sent and summed in bfloat16 or wider, within the bound.
No kernel may reach another device: no remote copies, remote signals or barrier semaphores. Data moves between devices by JAX's collectives and lax.ppermute only.
A program may use at most 64 MiB of HBM per device.

v0:
```python
import jax
import jax.numpy as jnp
from jax import lax
from jax.sharding import PartitionSpec as P

damping = 0.1


def contract(former, latter, former_dim, latter_dim):
    return lax.dot_general(
        former,
        latter,
        (((former_dim,), (latter_dim,)), ((), ())),
        preferred_element_type=jnp.float32,
    )


def over_rows(summands):
    return lax.psum(summands, "row")


def over_cols(summands):
    return lax.psum(summands, "col")


def shards(activations, gradients, act_basis, grad_basis, eigen_noise):
    token_count = activations.shape[0] * lax.axis_size("tok")
    basis_cols = lax.all_gather(act_basis, "tok", axis=1, tiled=True)
    act_proj = over_rows(contract(activations, basis_cols, 1, 0))
    grad_proj = over_cols(contract(gradients, grad_basis, 1, 0))
    act_sq = (act_proj * act_proj).astype(jnp.bfloat16)
    grad_sq = (grad_proj * grad_proj).astype(jnp.bfloat16)
    summed = lax.psum_scatter(
        contract(grad_sq, act_sq, 0, 0), "tok", scatter_dimension=1, tiled=True
    )
    scales = summed / token_count
    scaled = (eigen_noise * lax.rsqrt(token_count * (scales + damping))).astype(jnp.bfloat16)
    widened = lax.all_gather(scaled, "tok", axis=1, tiled=True)
    act_half = act_proj.astype(jnp.bfloat16)
    hidden = over_cols(contract(act_half, widened, 1, 1)).astype(jnp.bfloat16)
    output_shift = over_rows(contract(hidden, grad_basis, 1, 1)).astype(jnp.bfloat16)
    return (scales, output_shift)


def solution(mesh):
    in_specs = (
        P("tok", "row"),
        P("tok", "col"),
        P("row", ("tok", "col")),
        P("col", "row"),
        P("row", ("tok", "col")),
    )
    out_specs = (P("row", ("tok", "col")), P("tok", "col"))
    return jax.shard_map(shards, mesh=mesh, in_specs=in_specs, out_specs=out_specs, check_vma=False)
```

profile of v0, /device:TPU:1, one launch (start us, length us, event | category | flops | bytes accessed | tf_op | source)
XLA Modules:
  0.0 455.5 jit_solution(1851305855588722828)
XLA Ops:
  8.0 0.0 copy-start
  8.0 0.0 all-gather.3.cloned.1.call-start
  8.1 0.7 all-gather.3.cloned.1.call-update
  8.7 0.0 copy-start.1
  8.8 0.0 all-reduce.5.cloned.1.call-start
  8.8 0.8 copy-done
  9.6 2.7 fusion.5
  12.3 0.0 all-reduce.5.cloned.1.call-update
  12.4 0.0 all-reduce.7.cloned.1.call-start
  12.4 50.3 %all-gather.3.cloned.1.call-done = bf16[1024,1024]{1,0:T(8,128)(2,1)} async-done(((bf16[1024,128]{1,0:T(8,128)(2,1)}), bf16[1024,1024]{1,0:T(8,128)(2,1)}) %all-gather.3.cloned.1.call-update) | async-done | bytes 2097168 | tf_op jit(solution)/shard_map/all_gather | solution.py:28
  62.7 0.0 copy-done.1
  62.7 3.3 fusion.6
  66.0 0.0 all-reduce.7.cloned.1.call-update
  66.0 0.0 reduce-scatter.2.cloned.1.call-start
  66.0 38.1 %all-reduce.5.cloned.1.call-done = f32[256,1024]{1,0:T(8,128)} async-done(((f32[256,1024]{1,0:T(8,128)}), f32[256,1024]{1,0:T(8,128)}) %all-reduce.5.cloned.1.call-update) | async-done | bytes 1048592 | tf_op jit(solution)/shard_map/psum | solution.py:23
  104.1 88.2 %all-reduce.7.cloned.1.call-done = f32[256,1024]{1,0:T(8,128)} async-done(((f32[256,1024]{1,0:T(8,128)}), f32[256,1024]{1,0:T(8,128)}) %all-reduce.7.cloned.1.call-update) | async-done | bytes 1048592 | tf_op jit(solution)/shard_map/psum | solution.py:19
  192.3 4.2 fusion
  196.6 0.0 copy-start.2
  196.6 0.0 reduce-scatter.2.cloned.1.call-update
  196.6 0.0 all-gather.5.cloned.1.call-start
  196.6 58.6 %reduce-scatter.2.cloned.1.call-done = f32[1024,128]{1,0:T(8,128)} async-done(((f32[1024,1024]{1,0:T(8,128)}), f32[1024,128]{1,0:T(8,128)}) %reduce-scatter.2.cloned.1.call-update) | async-done | bytes 524304 | tf_op jit(solution)/shard_map/reduce_scatter | solution.py:33
  255.3 0.0 copy-done.2
  255.3 2.0 multiply_convert_fusion.4
  257.3 0.0 all-gather.5.cloned.1.call-update
  257.3 44.4 %all-gather.5.cloned.1.call-done = bf16[1024,1024]{1,0:T(8,128)(2,1)} async-done(((bf16[1024,128]{1,0:T(8,128)(2,1)}), bf16[1024,1024]{1,0:T(8,128)(2,1)}) %all-gather.5.cloned.1.call-update) | async-done | bytes 2097168 | tf_op jit(solution)/shard_map/all_gather | solution.py:38
  301.8 2.7 fusion.3
  304.4 63.2 %all-reduce.8 = bf16[256,1024]{1,0:T(8,128)(2,1)} all-reduce(f32[256,1024]{1,0:T(8,128)S(1)} %fusion.3), channel_id=1, replica_groups=mesh['tok'=8,'row'=8,'col'=8] {'col'}, use_global_device_ids=true, to_apply=%region_3.0 | all-reduce | flops 262144 | bytes 1572864 | tf_op jit(solution)/shard_map/psum | solution.py:23
  367.6 1.8 fusion.7
  369.4 79.0 %all-reduce.9 = bf16[256,1024]{1,0:T(8,128)(2,1)} all-reduce(f32[256,1024]{1,0:T(8,128)S(1)} %fusion.7), channel_id=1, replica_groups=mesh['tok'=8,'row'=8,'col'=8] {'row'}, use_global_device_ids=true, to_apply=%region_4.0 | all-reduce | flops 262144 | bytes 1572864 | tf_op jit(solution)/shard_map/psum | solution.py:19
Async XLA Ops:
  8.0 1.6 copy-start
  8.0 54.7 %all-gather.3.cloned.1.call-start = ((), (), s32[]{:S(2)}) async-start(), calls=%async_computation.2 | async-start | bytes 2359296 | tf_op jit(solution)/shard_map/all_gather | solution.py:28
  8.7 53.9 %copy-start.1 = (bf16[256,1024]{1,0:T(8,128)(2,1)S(1)}, bf16[256,1024]{1,0:T(8,128)(2,1)}, u32[]{:S(2)}) copy-start(bf16[256,1024]{1,0:T(8,128)(2,1)} %param.5) | copy-start | bytes 1572868
  8.8 95.3 %all-reduce.5.cloned.1.call-start = ((), (), s32[]{:S(2)}) async-start(), calls=%async_computation.1 | async-start | bytes 2097152 | tf_op jit(solution)/shard_map/psum | solution.py:23
  12.4 180.0 %all-reduce.7.cloned.1.call-start = ((), (), s32[]{:S(2)}) async-start(), calls=%async_computation.3 | async-start | bytes 2097152 | tf_op jit(solution)/shard_map/psum | solution.py:19
  66.0 189.3 %reduce-scatter.2.cloned.1.call-start = ((), (), s32[]{:S(2)}) async-start(), calls=%async_computation.4 | async-start | bytes 4718592 | tf_op jit(solution)/shard_map/reduce_scatter | solution.py:33
  196.6 58.7 %copy-start.2 = (f32[1024,128]{1,0:T(8,128)S(1)}, f32[1024,128]{1,0:T(8,128)}, u32[]{:S(2)}) copy-start(f32[1024,128]{1,0:T(8,128)} %param.9) | copy-start | bytes 1572868
  196.6 105.2 %all-gather.5.cloned.1.call-start = ((), (), s32[]{:S(2)}) async-start(), calls=%async_computation.5 | async-start | bytes 2359296 | tf_op jit(solution)/shard_map/all_gather | solution.py:38
Sparse Core Ops, SparseCore 0:
  10.8 51.8 all-gather.2
  196.7 58.5 reduce-scatter.1
  257.9 43.8 all-gather.4
Sparse Core Ops, SparseCore 1:
  12.4 91.6 all-reduce.4
  106.9 85.4 all-reduce.6
where the time goes:
time: 457 us; the launch traced here: 455 us
  waiting for transfers between devices  280 us (61%)
  blocking collectives  142 us (31%)
  between operations  15.2 us (3%)
  matrix products  14.7 us (3%)
    psum x1, waiting for transfers between devices, over_rows(): return lax.psum(summands, 'row')  88.2 us
    psum x1, blocking collectives, over_rows(): return lax.psum(summands, 'row')  79 us
    psum x1, blocking collectives, over_cols(): return lax.psum(summands, 'col')  63.2 us
    reduce_scatter x1, waiting for transfers between devices, shards(): lax.psum_scatter(contract(grad_sq, act_sq, 0, 0), 'tok', scatter_dimensio...  58.6 us
    all_gather x1, waiting for transfers between devices, shards(): basis_cols = lax.all_gather(act_basis, 'tok', axis=1, tiled=True)  50.3 us
    all_gather x1, waiting for transfers between devices, shards(): widened = lax.all_gather(scaled, 'tok', axis=1, tiled=True)  44.4 us
    psum x1, waiting for transfers between devices, over_cols(): return lax.psum(summands, 'col')  38.1 us
    dot_general x5, matrix products, contract(): lax.dot_general(former, latter, (((former_dim,), (latter_dim,)), ((), ())...  14.7 us
  transfers between devices with their start and end apart: 5, of which 5 were waited for; matrix products, arithmetic and copies ran while one was open for 1% of the time, Pallas kernels for 0%

commit v1 on v0

v1 whole, which is shorter than its diff:
```python
import jax
import jax.numpy as jnp
from jax import lax
from jax.sharding import Mesh, PartitionSpec as P

damping = 0.1
narrow = jnp.bfloat16
wide = jnp.float32
row = ("yh", "core")
col = ("x", "yl")


def contract(former, latter, former_dim, latter_dim):
    return lax.dot_general(
        former,
        latter,
        (((former_dim,), (latter_dim,)), ((), ())),
        preferred_element_type=wide,
    )


def exchange(blocks, axes):
    return lax.all_to_all(blocks, axes, 0, 0, tiled=True)


def spread(block, axes):
    members = lax.axis_size(axes)
    copies = jnp.broadcast_to(block[None], (members, *block.shape))
    return exchange(copies.reshape(members * block.shape[0], *block.shape[1:]), axes)


def scatter_sum(partial, axes):
    members = lax.axis_size(axes)
    parts = exchange(partial.astype(narrow), axes)
    parts = parts.reshape(members, parts.shape[0] // members, *parts.shape[1:])
    return jnp.sum(parts.astype(wide), axis=0)


def shards(activations, gradients, act_basis, grad_basis, eigen_noise):
    token_count = activations.shape[0] * lax.axis_size("tok")
    slab = activations.shape[0] // lax.axis_size("x")

    grad_proj = scatter_sum(contract(gradients, grad_basis, 1, 0), col)
    grad_sq = spread((grad_proj * grad_proj).astype(narrow), ("tok", "yl"))

    own_rows = lax.dynamic_slice_in_dim(activations, lax.axis_index("x") * slab, slab, 0)
    act_rows = spread(own_rows, "tok")
    basis_t = spread(act_basis.T, "x")
    act_proj = scatter_sum(contract(act_rows, basis_t, 1, 1), row)
    act_half = lax.all_gather(act_proj.astype(narrow), row, axis=0, tiled=True)
    act_wide = act_half.astype(wide)
    act_sq = (act_wide * act_wide).astype(narrow)

    scales_t = scatter_sum(contract(act_sq, grad_sq, 0, 0), "x") / token_count
    scaled_t = (eigen_noise.T * lax.rsqrt(token_count * (scales_t + damping))).astype(narrow)
    widened_t = spread(scaled_t, "x")

    hidden = scatter_sum(contract(act_half, widened_t, 1, 0), ("tok", "yl")).astype(narrow)
    hidden = spread(hidden, col)
    shift = scatter_sum(contract(hidden, grad_basis, 1, 1), row).astype(narrow)
    output_shift = lax.all_gather(shift, row, axis=0, tiled=True)
    return (scales_t.T, output_shift)


def solution(mesh):
    fine = Mesh(mesh.devices.reshape(8, 4, 2, 4, 2), ("tok", "yh", "core", "x", "yl"))
    in_specs = (
        P("tok", row),
        P("tok", col),
        P(row, ("tok", *col)),
        P(col, row),
        P(row, ("tok", *col)),
    )
    out_specs = (P(row, ("tok", *col)), P("tok", col))
    return jax.shard_map(shards, mesh=fine, in_specs=in_specs, out_specs=out_specs, check_vma=False)
```

time: 457 us -> 266 us (0.58)
  waiting for transfers between devices: 280 us -> 82.3 us
  starting transfers between devices: 0.21 us -> 46.5 us
  blocking collectives: 142 us -> 112 us
  between operations: 15.2 us -> 0.74 us
  local copies, waits for them, and re-layouts: 0.8 us -> 9.65 us
    psum x2 -> x0, blocking collectives: 142 us -> none  [the longest x1 79 us: over_rows(): return lax.psum(summands, 'row')]
    psum x2 -> x0, waiting for transfers between devices: 126 us -> none  [the longest x1 88.2 us: over_rows(): return lax.psum(summands, 'row')]
    all_gather x2 -> x0, waiting for transfers between devices: 94.7 us -> none  [the longest x1 50.3 us: shards(): basis_cols = lax.all_gather(act_basis, 'tok', axis=1, tiled=True)]
    all_to_all x0 -> x7, waiting for transfers between devices: none -> 82.3 us  [exchange(): return lax.all_to_all(blocks, axes, 0, 0, tiled=True)]
    all_to_all x0 -> x3, blocking collectives: none -> 62.9 us  [exchange(): return lax.all_to_all(blocks, axes, 0, 0, tiled=True)]
    reduce_scatter x1 -> x0, waiting for transfers between devices: 58.6 us -> none  [shards(): lax.psum_scatter(contract(grad_sq, act_sq, 0, 0), 'tok', scatter_dimensio...]
    all_gather x0 -> x2, blocking collectives: none -> 49.3 us  [the longest x1 30.9 us: shards(): act_half = lax.all_gather(act_proj.astype(narrow), row, axis=0, tiled=True)]
    all_to_all x0 -> x7, starting transfers between devices: none -> 46.5 us  [exchange(): return lax.all_to_all(blocks, axes, 0, 0, tiled=True)]
  transfers between devices with their start and end apart: 5 -> 7, of which waited for: 5 -> 6; matrix products, arithmetic and copies ran while one was open for 1% -> 4% of each run, Pallas kernels for 0% -> 0%
where the time goes in v1:
time: 266 us; the launch traced here: 265 us
  blocking collectives  112 us (42%)
  waiting for transfers between devices  82.3 us (31%)
  starting transfers between devices  46.5 us (17%)
  matrix products  11 us (4%)
  local copies, waits for them, and re-layouts  9.65 us (4%)
    all_to_all x7, waiting for transfers between devices, exchange(): return lax.all_to_all(blocks, axes, 0, 0, tiled=True)  82.3 us
    all_to_all x3, blocking collectives, exchange(): return lax.all_to_all(blocks, axes, 0, 0, tiled=True)  62.9 us
    all_to_all x7, starting transfers between devices, exchange(): return lax.all_to_all(blocks, axes, 0, 0, tiled=True)  46.5 us
    all_gather x1, blocking collectives, shards(): act_half = lax.all_gather(act_proj.astype(narrow), row, axis=0, tiled=True)  30.9 us
    all_gather x1, blocking collectives, shards(): output_shift = lax.all_gather(shift, row, axis=0, tiled=True)  18.4 us
    dot_general x5, matrix products, contract(): lax.dot_general(former, latter, (((former_dim,), (latter_dim,)), ((), ())...  11 us
  transfers between devices with their start and end apart: 7, of which 6 were waited for; matrix products, arithmetic and copies ran while one was open for 4% of the time, Pallas kernels for 0%

profile of v1, /device:TPU:1, one launch (start us, length us, event | category | flops | bytes accessed | tf_op | source)
XLA Modules:
  0.0 265.0 jit_solution(674721153506149735)
XLA Ops:
  0.6 0.0 copy-start
  0.6 1.2 copy.9
  1.9 1.1 broadcast_in_dim.11
  3.0 4.8 %all-to-all-start.1 = ((bf16[4,128,1024]{2,1,0:T(8,128)(2,1)}), bf16[4,128,1024]{2,1,0:T(8,128)(2,1)S(1)}, u32[]{:S(2)}, u32[]{:S(2)}) async-start(bf16[4,128,1024]{2,1,0:T(8,128)(2,1)} %broadcast_in_dim.11), calls=%async_computation.1 | async-start | bytes 2097152 | tf_op jit(solution)/shard_map/all_to_all | solution.py:23
  7.8 0.9 constant_dynamic-slice_fusion
  8.7 8.8 %all-to-all-done.1 = bf16[4,128,1024]{2,1,0:T(8,128)(2,1)S(1)} async-done(((bf16[4,128,1024]{2,1,0:T(8,128)(2,1)}), bf16[4,128,1024]{2,1,0:T(8,128)(2,1)S(1)}, u32[]{:S(2)}, u32[]{:S(2)}) %all-to-all-start.1) | async-done | bytes 1048608 | tf_op jit(solution)/shard_map/all_to_all | solution.py:23
  17.6 0.0 copy-start.2
  17.6 1.2 broadcast_in_dim.10
  18.8 14.5 %all-to-all-start = ((bf16[8,64,1024]{2,1,0:T(8,128)(2,1)}), bf16[8,64,1024]{2,1,0:T(8,128)(2,1)}, u32[]{:S(2)}, u32[]{:S(2)}) async-start(bf16[8,64,1024]{2,1,0:T(8,128)(2,1)} %broadcast_in_dim.10), calls=%async_computation | async-start | bytes 2097152 | tf_op jit(solution)/shard_map/all_to_all | solution.py:23
  33.3 0.0 copy-done
  33.3 2.5 convolution_convert_fusion.3
  35.9 0.0 copy-done.2
  35.9 26.7 %all-to-all-done = bf16[8,64,1024]{2,1,0:T(8,128)(2,1)} async-done(((bf16[8,64,1024]{2,1,0:T(8,128)(2,1)}), bf16[8,64,1024]{2,1,0:T(8,128)(2,1)}, u32[]{:S(2)}, u32[]{:S(2)}) %all-to-all-start) | async-done | bytes 1048608 | tf_op jit(solution)/shard_map/all_to_all | solution.py:23
  62.6 3.5 %all-to-all-start.3 = ((bf16[8,32,1024]{2,1,0:T(8,128)(2,1)}), bf16[8,32,1024]{2,1,0:T(8,128)(2,1)S(1)}, u32[]{:S(2)}, u32[]{:S(2)}) async-start(bf16[8,32,1024]{2,1,0:T(8,128)(2,1)} %bitcast.31), calls=%async_computation.3 | async-start | bytes 1048576 | tf_op jit(solution)/shard_map/all_to_all | solution.py:23
  66.1 3.1 %convolution_convert_fusion.4 = bf16[512,512]{1,0:T(8,128)(2,1)} fusion(bf16[512,1024]{1,0:T(8,128)(2,1)} %bitcast, bf16[512,1024]{1,0:T(8,128)(2,1)} %bitcast.26), kind=kOutput, calls=%fused_computation.5 | convolution fusion | flops 537133056 | bytes 2621440 | tf_op jit(solution)/shard_map/dot_general | solution.py:14
  69.2 6.2 %all-to-all-done.3 = bf16[8,32,1024]{2,1,0:T(8,128)(2,1)S(1)} async-done(((bf16[8,32,1024]{2,1,0:T(8,128)(2,1)}), bf16[8,32,1024]{2,1,0:T(8,128)(2,1)S(1)}, u32[]{:S(2)}, u32[]{:S(2)}) %all-to-all-start.3) | async-done | bytes 524320 | tf_op jit(solution)/shard_map/all_to_all | solution.py:23
  75.4 8.8 %all-to-all-start.2 = ((bf16[8,64,512]{2,1,0:T(8,128)(2,1)}), bf16[8,64,512]{2,1,0:T(8,128)(2,1)S(1)}, u32[]{:S(2)}, u32[]{:S(2)}) async-start(bf16[8,64,512]{2,1,0:T(8,128)(2,1)} %bitcast.30), calls=%async_computation.2 | async-start | bytes 1048576 | tf_op jit(solution)/shard_map/all_to_all | solution.py:23
  84.2 0.1 convert_reduce_fusion.1
  84.3 14.2 %all-to-all-done.2 = bf16[8,64,512]{2,1,0:T(8,128)(2,1)S(1)} async-done(((bf16[8,64,512]{2,1,0:T(8,128)(2,1)}), bf16[8,64,512]{2,1,0:T(8,128)(2,1)S(1)}, u32[]{:S(2)}, u32[]{:S(2)}) %all-to-all-start.2) | async-done | bytes 524320 | tf_op jit(solution)/shard_map/all_to_all | solution.py:23
  98.5 1.1 broadcast_in_dim.12
  99.7 4.3 %all-to-all-start.4 = ((bf16[16,32,1024]{2,1,0:T(8,128)(2,1)}), bf16[16,32,1024]{2,1,0:T(8,128)(2,1)}, u32[]{:S(2)}, u32[]{:S(2)}) async-start(bf16[16,32,1024]{2,1,0:T(8,128)(2,1)} %broadcast_in_dim.12), calls=%async_computation.4 | async-start | bytes 2097152 | tf_op jit(solution)/shard_map/all_to_all | solution.py:23
  104.0 0.1 reduce_sum.54
  104.1 30.9 %all_gather.6 = bf16[512,512]{1,0:T(8,128)(2,1)S(1)} all-gather(bf16[64,512]{1,0:T(8,128)(2,1)S(1)} %reduce_sum.54), channel_id=1, replica_groups=mesh['tok'=8,'yh'=4,'core'=2,'x'=4,'yl'=2] {'yh','core'}, dimensions={0}, use_global_device_ids=true | all-gather | bytes 589824 | tf_op jit(solution)/shard_map/all_gather | solution.py:50
  135.0 0.0 copy-start.3
  135.0 0.0 all-to-all-done.4
  135.0 3.2 %convolution_convert_fusion.1 = bf16[512,1024]{1,0:T(8,128)(2,1)} fusion(bf16[512,1024]{1,0:T(8,128)(2,1)} %bitcast.5, bf16[512,512]{1,0:T(8,128)(2,1)S(1)} %all_gather.6), kind=kOutput, calls=%fused_computation.2 | convolution fusion | flops 538181632 | bytes 2621440 | tf_op jit(solution)/shard_map/dot_general | solution.py:14
  138.2 0.0 copy-done.3
  138.2 3.5 %all-to-all-start.5 = ((bf16[4,128,1024]{2,1,0:T(8,128)(2,1)}), bf16[4,128,1024]{2,1,0:T(8,128)(2,1)S(1)}, u32[]{:S(2)}, u32[]{:S(2)}) async-start(bf16[4,128,1024]{2,1,0:T(8,128)(2,1)} %bitcast.27), calls=%async_computation.5 | async-start | bytes 2097152 | tf_op jit(solution)/shard_map/all_to_all | solution.py:23
  141.7 2.0 copy.10
  143.8 13.0 %all-to-all-done.5 = bf16[4,128,1024]{2,1,0:T(8,128)(2,1)S(1)} async-done(((bf16[4,128,1024]{2,1,0:T(8,128)(2,1)}), bf16[4,128,1024]{2,1,0:T(8,128)(2,1)S(1)}, u32[]{:S(2)}, u32[]{:S(2)}) %all-to-all-start.5) | async-done | bytes 1048608 | tf_op jit(solution)/shard_map/all_to_all | solution.py:23
  156.7 0.2 convert_reduce_fusion
  156.9 1.9 fusion
  158.9 0.0 copy-start.4
  158.9 0.1 broadcast_in_dim.13
  159.0 16.7 %all_to_all.90 = bf16[4,128,1024]{2,1,0:T(8,128)(2,1)S(1)} all-to-all(bf16[4,128,1024]{2,1,0:T(8,128)(2,1)S(1)} %broadcast_in_dim.13), channel_id=1, replica_groups=mesh['tok'=8,'yh'=4,'core'=2,'x'=4,'yl'=2] {'x'}, dimensions={0} | all-to-all | bytes 2097152 | tf_op jit(solution)/shard_map/all_to_all | solution.py:23
  175.7 0.0 copy-done.4
  175.7 0.7 convolution_convert_fusion
  176.4 33.4 %all_to_all.91 = bf16[16,32,1024]{2,1,0:T(8,128)(2,1)S(1)} all-to-all(bf16[16,32,1024]{2,1,0:T(8,128)(2,1)S(1)} %bitcast.29), channel_id=1, replica_groups=mesh['tok'=8,'yh'=4,'core'=2,'x'=4,'yl'=2] {'tok','yl'}, dimensions={0} | all-to-all | bytes 2097152 | tf_op jit(solution)/shard_map/all_to_all | solution.py:23
  209.9 0.2 reduce_sum.57
  210.1 0.1 broadcast_in_dim.14
  210.1 12.8 %all_to_all.92 = bf16[8,32,1024]{2,1,0:T(8,128)(2,1)S(1)} all-to-all(bf16[8,32,1024]{2,1,0:T(8,128)(2,1)S(1)} %broadcast_in_dim.14), channel_id=1, replica_groups=mesh['tok'=8,'yh'=4,'core'=2,'x'=4,'yl'=2] {'x','yl'}, dimensions={0} | all-to-all | bytes 1048576 | tf_op jit(solution)/shard_map/all_to_all | solution.py:23
  222.9 0.0 copy-start.1
  222.9 1.5 convolution_convert_fusion.2
  224.4 7.0 %all-to-all-start.9 = ((bf16[8,32,1024]{2,1,0:T(8,128)(2,1)}), bf16[8,32,1024]{2,1,0:T(8,128)(2,1)S(1)}, u32[]{:S(2)}, u32[]{:S(2)}) async-start(bf16[8,32,1024]{2,1,0:T(8,128)(2,1)} %bitcast.32), calls=%async_computation.9 | async-start | bytes 1048576 | tf_op jit(solution)/shard_map/all_to_all | solution.py:23
  231.4 0.0 copy-done.1
  231.4 1.0 copy.11
  232.4 13.3 %all-to-all-done.9 = bf16[8,32,1024]{2,1,0:T(8,128)(2,1)S(1)} async-done(((bf16[8,32,1024]{2,1,0:T(8,128)(2,1)}), bf16[8,32,1024]{2,1,0:T(8,128)(2,1)S(1)}, u32[]{:S(2)}, u32[]{:S(2)}) %all-to-all-start.9) | async-done | bytes 524320 | tf_op jit(solution)/shard_map/all_to_all | solution.py:23
  245.7 0.1 reduce_sum.58
  245.8 18.4 %all_gather.7 = bf16[256,1024]{1,0:T(8,128)(2,1)S(1)} all-gather(bf16[32,1024]{1,0:T(8,128)(2,1)S(1)} %reduce_sum.58), channel_id=1, replica_groups=mesh['tok'=8,'yh'=4,'core'=2,'x'=4,'yl'=2] {'yh','core'}, dimensions={0}, use_global_device_ids=true | all-gather | bytes 589824 | tf_op jit(solution)/shard_map/all_gather | solution.py:61
  264.2 0.8 copy.13
  (1 shorter events, 0.0 us)
Async XLA Ops:
  0.6 32.7 %copy-start = (bf16[1024,1024]{1,0:T(8,128)(2,1)S(1)}, bf16[1024,1024]{1,0:T(8,128)(2,1)}, u32[]{:S(2)}) copy-start(bf16[1024,1024]{1,0:T(8,128)(2,1)} %param.8) | copy-start | bytes 6291460
  3.0 14.6 %all-to-all-start.1 = ((bf16[4,128,1024]{2,1,0:T(8,128)(2,1)}), bf16[4,128,1024]{2,1,0:T(8,128)(2,1)S(1)}, u32[]{:S(2)}, u32[]{:S(2)}) async-start(bf16[4,128,1024]{2,1,0:T(8,128)(2,1)} %broadcast_in_dim.11), calls=%async_computation.1 | async-start | bytes 2097152 | tf_op jit(solution)/shard_map/all_to_all | solution.py:23
  17.6 18.3 %copy-start.2 = (bf16[4,128,1024]{2,1,0:T(8,128)(2,1)}, bf16[4,128,1024]{2,1,0:T(8,128)(2,1)S(1)}, u32[]{:S(2)}) copy-start(bf16[4,128,1024]{2,1,0:T(8,128)(2,1)S(1)} %all-to-all-done.1) | copy-start | bytes 3145732
  18.8 43.8 %all-to-all-start = ((bf16[8,64,1024]{2,1,0:T(8,128)(2,1)}), bf16[8,64,1024]{2,1,0:T(8,128)(2,1)}, u32[]{:S(2)}, u32[]{:S(2)}) async-start(bf16[8,64,1024]{2,1,0:T(8,128)(2,1)} %broadcast_in_dim.10), calls=%async_computation | async-start | bytes 2097152 | tf_op jit(solution)/shard_map/all_to_all | solution.py:23
  62.6 12.8 %all-to-all-start.3 = ((bf16[8,32,1024]{2,1,0:T(8,128)(2,1)}), bf16[8,32,1024]{2,1,0:T(8,128)(2,1)S(1)}, u32[]{:S(2)}, u32[]{:S(2)}) async-start(bf16[8,32,1024]{2,1,0:T(8,128)(2,1)} %bitcast.31), calls=%async_computation.3 | async-start | bytes 1048576 | tf_op jit(solution)/shard_map/all_to_all | solution.py:23
  75.4 23.1 %all-to-all-start.2 = ((bf16[8,64,512]{2,1,0:T(8,128)(2,1)}), bf16[8,64,512]{2,1,0:T(8,128)(2,1)S(1)}, u32[]{:S(2)}, u32[]{:S(2)}) async-start(bf16[8,64,512]{2,1,0:T(8,128)(2,1)} %bitcast.30), calls=%async_computation.2 | async-start | bytes 1048576 | tf_op jit(solution)/shard_map/all_to_all | solution.py:23
  99.7 35.3 %all-to-all-start.4 = ((bf16[16,32,1024]{2,1,0:T(8,128)(2,1)}), bf16[16,32,1024]{2,1,0:T(8,128)(2,1)}, u32[]{:S(2)}, u32[]{:S(2)}) async-start(bf16[16,32,1024]{2,1,0:T(8,128)(2,1)} %broadcast_in_dim.12), calls=%async_computation.4 | async-start | bytes 2097152 | tf_op jit(solution)/shard_map/all_to_all | solution.py:23
  135.0 3.2 %copy-start.3 = (bf16[512,512]{1,0:T(8,128)(2,1)}, bf16[512,512]{1,0:T(8,128)(2,1)S(1)}, u32[]{:S(2)}) copy-start(bf16[512,512]{1,0:T(8,128)(2,1)S(1)} %all_gather.6) | copy-start | bytes 1572868
  138.2 18.5 %all-to-all-start.5 = ((bf16[4,128,1024]{2,1,0:T(8,128)(2,1)}), bf16[4,128,1024]{2,1,0:T(8,128)(2,1)S(1)}, u32[]{:S(2)}, u32[]{:S(2)}) async-start(bf16[4,128,1024]{2,1,0:T(8,128)(2,1)} %bitcast.27), calls=%async_computation.5 | async-start | bytes 2097152 | tf_op jit(solution)/shard_map/all_to_all | solution.py:23
  158.9 16.9 %copy-start.4 = (bf16[512,512]{1,0:T(8,128)(2,1)S(1)}, bf16[512,512]{1,0:T(8,128)(2,1)}, u32[]{:S(2)}) copy-start(bf16[512,512]{1,0:T(8,128)(2,1)} %copy-done.3) | copy-start | bytes 1572868
  222.9 8.5 %copy-start.1 = (f32[1024,128]{0,1:T(8,128)S(1)}, f32[1024,128]{0,1:T(8,128)}, u32[]{:S(2)}) copy-start(f32[1024,128]{0,1:T(8,128)} %get-tuple-element.5) | copy-start | bytes 1572868
  224.4 21.3 %all-to-all-start.9 = ((bf16[8,32,1024]{2,1,0:T(8,128)(2,1)}), bf16[8,32,1024]{2,1,0:T(8,128)(2,1)S(1)}, u32[]{:S(2)}, u32[]{:S(2)}) async-start(bf16[8,32,1024]{2,1,0:T(8,128)(2,1)} %bitcast.32), calls=%async_computation.9 | async-start | bytes 1048576 | tf_op jit(solution)/shard_map/all_to_all | solution.py:23
